TPU v7x, 32 devices: a whole 2x2x4 slice. The times are simulated.
32 devices in a mesh: seq: 2 (over y), fsdp: 16 (over z, x, core).
Axes of the slice: x: 2, y: 2, z: 4, core: 2. Of those that a mesh axis runs over, the one named last changes fastest.
Arguments:
- tokens: bfloat16 [16, 1024, 1024], P('fsdp', 'seq'), may hold values from -6 to 6
- blocks: int32 [16, 1024], P('fsdp'), may hold values from 0 to 7, never falling along the last dimension, each value on 1 to 256 neighbouring positions
- first_gain: bfloat16 [1024], P('fsdp'), may hold values from 0.5 to 1.5
- first_shift: bfloat16 [1024], P('fsdp'), may hold values from -1.5 to 1.5
- joint_weight: bfloat16 [1024, 3072], P('fsdp'), may hold values from -0.1875 to 0.1875
- joint_bias: bfloat16 [2, 1024], P(None, 'fsdp'), may hold values from -1.5 to 1.5
- output_weight: bfloat16 [1024, 1024], P('fsdp'), may hold values from -0.75 to 0.75
- output_bias: bfloat16 [1024], P('fsdp'), may hold values from -1.5 to 1.5
- second_gain: bfloat16 [1024], P('fsdp'), may hold values from 0.5 to 1.5
- second_shift: bfloat16 [1024], P('fsdp'), may hold values from -1.5 to 1.5
- upward_weight: bfloat16 [1024, 4096], P('fsdp'), may hold values from -0.1875 to 0.1875
- upward_bias: bfloat16 [4096], P('fsdp'), may hold values from -1.5 to 1.5
- downward_weight: bfloat16 [4096, 1024], P('fsdp'), may hold values from -0.125 to 0.125
- downward_bias: bfloat16 [1024], P('fsdp'), may hold values from -1.5 to 1.5
- cotangent: bfloat16 [16, 1024, 1024], P('fsdp', 'seq'), may hold values from -6 to 6
Outputs:
- result: bfloat16 [16, 1024, 1024], P('fsdp', 'seq')
- grad_tokens: float32 [16, 1024, 1024], P('fsdp', 'seq')
- grad_first_gain: float32 [1024], P('fsdp')
- grad_first_shift: float32 [1024], P('fsdp')
- grad_joint_weight: float32 [1024, 3072], P('fsdp')
- grad_joint_bias: float32 [2, 1024], P(None, 'fsdp')
- grad_output_weight: float32 [1024, 1024], P('fsdp')
- grad_output_bias: float32 [1024], P('fsdp')
- grad_second_gain: float32 [1024], P('fsdp')
- grad_second_shift: float32 [1024], P('fsdp')
- grad_upward_weight: float32 [1024, 4096], P('fsdp')
- grad_upward_bias: float32 [4096], P('fsdp')
- grad_downward_weight: float32 [4096, 1024], P('fsdp')
- grad_downward_bias: float32 [1024], P('fsdp')
Inputs may be any that keep to these rules, and one draw needn't show every extreme that they name: `blocks`: along each sequence the block number never falls; every block has 1 to 256 tokens, and one has exactly 256.
All inputs are finite; a program needn't handle non-finite values.
Results may differ from a plain program's by a relative error of at most 0.014.
Values may be sent and summed in bfloat16 or wider, within the bound.
No kernel may reach another device: no remote copies, remote signals or barrier semaphores. Data moves between devices by JAX's collectives and lax.ppermute only.
A program may use at most 192 MiB of HBM per device.

v0:
```python
import jax
import jax.numpy as jnp
from jax import lax
from jax.sharding import PartitionSpec as P

HEADS = 16
HEAD_DIM = 64
EPSILON = 1e-05


def scaled_norm(values, gain):
    center = values - jnp.mean(values, axis=-1, keepdims=True)
    spread = jnp.mean(center * center, axis=-1, keepdims=True)
    return center * lax.rsqrt(spread + EPSILON) * gain


def gelu_tanh(values):
    return jax.nn.gelu(values, approximate=True)


def matmul(left, right):
    return jnp.dot(left, right, preferred_element_type=jnp.float32)


def left_contract(left, right):
    return lax.dot_general(
        left, right, (((0,), (0,)), ((), ())), preferred_element_type=jnp.float32
    )


def right_contract(left, right):
    return lax.dot_general(
        left, right, (((1,), (1,)), ((), ())), preferred_element_type=jnp.float32
    )


def masked_scores(queries, keys_in, slope, distance, allowed):
    scores = right_contract(queries, keys_in) * HEAD_DIM ** (-0.5) - slope * distance
    return jnp.where(allowed, scores, -1e30)


def attend_heads(heads, slopes, distance, allowed):

    def one_head(packed):
        queries, keys_in, values_in, slope = packed
        scores = masked_scores(queries, keys_in, slope, distance, allowed)
        top_score = jnp.max(scores, axis=1, keepdims=True)
        totals = jnp.sum(jnp.exp(scores - top_score), axis=1, keepdims=True)
        log_total = top_score + jnp.log(totals)
        probs = jnp.exp(scores - log_total).astype(jnp.bfloat16)
        return (matmul(probs, values_in).astype(jnp.bfloat16), log_total[:, 0])

    return lax.map(one_head, (heads[0], heads[1], heads[2], slopes))


def attend_back(heads, log_totals, grad_heads, slopes, distance, allowed):

    def one_head(packed):
        queries, keys_in, values_in, log_total, grad_head, slope = packed
        scores = masked_scores(queries, keys_in, slope, distance, allowed)
        probs = jnp.exp(scores - log_total[:, None])
        grad_probs = right_contract(grad_head, values_in)
        inner = jnp.sum(probs * grad_probs, axis=1, keepdims=True)
        grad_scores = (probs * (grad_probs - inner)).astype(jnp.bfloat16)
        factor = HEAD_DIM ** (-0.5)
        grad_queries = matmul(grad_scores, keys_in) * factor
        grad_keys = left_contract(grad_scores, queries) * factor
        grad_values = left_contract(probs.astype(jnp.bfloat16), grad_head)
        return jnp.stack([grad_queries, grad_keys, grad_values]).astype(jnp.bfloat16)

    return lax.map(one_head, (heads[0], heads[1], heads[2], log_totals, grad_heads, slopes))


def per_device(
    tokens,
    blocks,
    first_gain,
    first_shift,
    joint_weight,
    joint_bias,
    output_weight,
    output_bias,
    second_gain,
    second_shift,
    upward_weight,
    upward_bias,
    downward_weight,
    downward_bias,
    cotangent,
):
    groups = lax.axis_size("seq")
    token_count = tokens.shape[1]
    model_width = tokens.shape[2]
    seq_length = token_count * groups
    local_heads = HEADS // groups
    group_width = model_width // groups
    inputs = tokens[0].astype(jnp.float32)
    attn_set = (
        lax.all_gather(first_gain, "fsdp", axis=0, tiled=True),
        lax.all_gather(first_shift, "fsdp", axis=0, tiled=True),
        lax.all_gather(joint_weight, "fsdp", axis=0, tiled=True),
        lax.all_gather(joint_bias, "fsdp", axis=1, tiled=True),
        lax.all_gather(output_weight, "fsdp", axis=0, tiled=True),
        lax.all_gather(output_bias, "fsdp", axis=0, tiled=True),
    )
    normed_one = (
        scaled_norm(inputs, attn_set[0].astype(jnp.float32)) + attn_set[1].astype(jnp.float32)
    ).astype(jnp.bfloat16)
    bias_full = jnp.concatenate(
        [attn_set[3][0], jnp.zeros((model_width,), jnp.bfloat16), attn_set[3][1]]
    ).astype(jnp.float32)
    joint = (matmul(normed_one, attn_set[2]) + bias_full).astype(jnp.bfloat16)
    joint = joint.reshape(token_count, 3, groups, group_width)
    heads = lax.all_to_all(joint, "seq", split_axis=2, concat_axis=0, tiled=True)
    heads = heads.reshape(seq_length, 3, local_heads, HEAD_DIM).transpose(1, 2, 0, 3)
    positions = jnp.arange(seq_length)
    distance = jnp.abs(positions[:, None] - positions[None, :]).astype(jnp.float32)
    block_row = blocks[0]
    allowed = block_row[None, :] <= block_row[:, None]
    head_index = lax.axis_index("seq") * local_heads + jnp.arange(local_heads)
    slopes = jnp.exp2(-8.0 * (head_index.astype(jnp.float32) + 1.0) / HEADS)
    attended, log_totals = attend_heads(heads, slopes, distance, allowed)
    flat_heads = attended.transpose(1, 0, 2).reshape(seq_length, 1, group_width)
    mixed = lax.all_to_all(flat_heads, "seq", split_axis=0, concat_axis=1, tiled=True).reshape(
        token_count, model_width
    )
    hidden = inputs + matmul(mixed, attn_set[4]) + attn_set[5].astype(jnp.float32)
    mlp_set = (
        lax.all_gather(second_gain, "fsdp", axis=0, tiled=True),
        lax.all_gather(second_shift, "fsdp", axis=0, tiled=True),
        lax.all_gather(upward_weight, "fsdp", axis=0, tiled=True),
        lax.all_gather(upward_bias, "fsdp", axis=0, tiled=True),
        lax.all_gather(downward_weight, "fsdp", axis=0, tiled=True),
        lax.all_gather(downward_bias, "fsdp", axis=0, tiled=True),
    )
    normed_two = (
        scaled_norm(hidden, mlp_set[0].astype(jnp.float32)) + mlp_set[1].astype(jnp.float32)
    ).astype(jnp.bfloat16)
    upward = matmul(normed_two, mlp_set[2]) + mlp_set[3].astype(jnp.float32)
    activated = gelu_tanh(upward).astype(jnp.bfloat16)
    output = hidden + matmul(activated, mlp_set[4]) + mlp_set[5].astype(jnp.float32)
    back_gain_two, back_upward, back_downward = (
        lax.all_gather(second_gain, "fsdp", axis=0, tiled=True),
        lax.all_gather(upward_weight, "fsdp", axis=0, tiled=True),
        lax.all_gather(downward_weight, "fsdp", axis=0, tiled=True),
    )
    grad_output = cotangent[0].astype(jnp.float32)
    grad_low = grad_output.astype(jnp.bfloat16)
    grad_down_bias = jnp.sum(grad_low.astype(jnp.float32), axis=0)
    grad_down_weight = left_contract(activated, grad_low)
    grad_act = right_contract(grad_low, back_downward)
    gelu_back = jax.vjp(gelu_tanh, upward)[1]
    grad_up = gelu_back(grad_act)[0].astype(jnp.bfloat16)
    grad_up_bias = jnp.sum(grad_up.astype(jnp.float32), axis=0)
    grad_up_weight = left_contract(normed_two, grad_up)
    grad_normed_two = right_contract(grad_up, back_upward)
    norm_two_back = jax.vjp(scaled_norm, hidden, back_gain_two.astype(jnp.float32))[1]
    grad_hidden_norm, grad_gain_two = norm_two_back(grad_normed_two)
    grad_shift_two = jnp.sum(grad_normed_two, axis=0)
    grad_hidden = grad_output + grad_hidden_norm
    back_gain_one, back_joint, back_output = (
        lax.all_gather(first_gain, "fsdp", axis=0, tiled=True),
        lax.all_gather(joint_weight, "fsdp", axis=0, tiled=True),
        lax.all_gather(output_weight, "fsdp", axis=0, tiled=True),
    )
    hidden_low = grad_hidden.astype(jnp.bfloat16)
    grad_out_bias = jnp.sum(hidden_low.astype(jnp.float32), axis=0)
    grad_out_weight = left_contract(mixed, hidden_low)
    grad_mixed = right_contract(hidden_low, back_output).astype(jnp.bfloat16)
    grad_mixed = grad_mixed.reshape(token_count, groups, group_width)
    grad_heads = lax.all_to_all(grad_mixed, "seq", split_axis=1, concat_axis=0, tiled=True)
    grad_heads = grad_heads.reshape(seq_length, local_heads, HEAD_DIM).transpose(1, 0, 2)
    grad_stack = attend_back(heads, log_totals, grad_heads, slopes, distance, allowed)
    grad_stack = grad_stack.transpose(2, 1, 0, 3).reshape(seq_length, 3, 1, group_width)
    grad_joint = lax.all_to_all(grad_stack, "seq", split_axis=0, concat_axis=2, tiled=True)
    grad_joint = grad_joint.reshape(token_count, 3 * model_width)
    joint_sums = jnp.sum(grad_joint.astype(jnp.float32), axis=0)
    grad_joint_bias = jnp.stack([joint_sums[:model_width], joint_sums[2 * model_width :]])
    grad_joint_weight = left_contract(normed_one, grad_joint)
    grad_normed_one = right_contract(grad_joint, back_joint)
    norm_one_back = jax.vjp(scaled_norm, inputs, back_gain_one.astype(jnp.float32))[1]
    grad_input_norm, grad_gain_one = norm_one_back(grad_normed_one)
    grad_shift_one = jnp.sum(grad_normed_one, axis=0)
    grad_inputs = grad_hidden + grad_input_norm
    every_sum = (
        lax.psum_scatter(grad_gain_one, "fsdp", scatter_dimension=0, tiled=True),
        lax.psum_scatter(grad_shift_one, "fsdp", scatter_dimension=0, tiled=True),
        lax.psum_scatter(grad_joint_weight, "fsdp", scatter_dimension=0, tiled=True),
        lax.psum_scatter(grad_joint_bias, "fsdp", scatter_dimension=1, tiled=True),
        lax.psum_scatter(grad_out_weight, "fsdp", scatter_dimension=0, tiled=True),
        lax.psum_scatter(grad_out_bias, "fsdp", scatter_dimension=0, tiled=True),
        lax.psum_scatter(grad_gain_two, "fsdp", scatter_dimension=0, tiled=True),
        lax.psum_scatter(grad_shift_two, "fsdp", scatter_dimension=0, tiled=True),
        lax.psum_scatter(grad_up_weight, "fsdp", scatter_dimension=0, tiled=True),
        lax.psum_scatter(grad_up_bias, "fsdp", scatter_dimension=0, tiled=True),
        lax.psum_scatter(grad_down_weight, "fsdp", scatter_dimension=0, tiled=True),
        lax.psum_scatter(grad_down_bias, "fsdp", scatter_dimension=0, tiled=True),
    )
    attn_sums = every_sum[:6]
    mlp_sums = every_sum[6:]
    totals = (
        lax.psum(attn_sums[0].astype(jnp.bfloat16), "seq").astype(jnp.float32),
        lax.psum(attn_sums[1].astype(jnp.bfloat16), "seq").astype(jnp.float32),
        lax.psum(attn_sums[2].astype(jnp.bfloat16), "seq").astype(jnp.float32),
        lax.psum(attn_sums[3].astype(jnp.bfloat16), "seq").astype(jnp.float32),
        lax.psum(attn_sums[4].astype(jnp.bfloat16), "seq").astype(jnp.float32),
        lax.psum(attn_sums[5].astype(jnp.bfloat16), "seq").astype(jnp.float32),
        lax.psum(mlp_sums[0].astype(jnp.bfloat16), "seq").astype(jnp.float32),
        lax.psum(mlp_sums[1].astype(jnp.bfloat16), "seq").astype(jnp.float32),
        lax.psum(mlp_sums[2].astype(jnp.bfloat16), "seq").astype(jnp.float32),
        lax.psum(mlp_sums[3].astype(jnp.bfloat16), "seq").astype(jnp.float32),
        lax.psum(mlp_sums[4].astype(jnp.bfloat16), "seq").astype(jnp.float32),
        lax.psum(mlp_sums[5].astype(jnp.bfloat16), "seq").astype(jnp.float32),
    )
    return (
        output.astype(jnp.bfloat16)[None],
        grad_inputs[None],
        totals[0],
        totals[1],
        totals[2],
        totals[3],
        totals[4],
        totals[5],
        totals[6],
        totals[7],
        totals[8],
        totals[9],
        totals[10],
        totals[11],
    )


def solution(mesh):
    in_specs = (
        P("fsdp", "seq", None),
        P("fsdp", None),
        P("fsdp"),
        P("fsdp"),
        P("fsdp", None),
        P(None, "fsdp"),
        P("fsdp", None),
        P("fsdp"),
        P("fsdp"),
        P("fsdp"),
        P("fsdp", None),
        P("fsdp"),
        P("fsdp", None),
        P("fsdp"),
        P("fsdp", "seq", None),
    )
    out_specs = (
        P("fsdp", "seq", None),
        P("fsdp", "seq", None),
        P("fsdp"),
        P("fsdp"),
        P("fsdp", None),
        P(None, "fsdp"),
        P("fsdp", None),
        P("fsdp"),
        P("fsdp"),
        P("fsdp"),
        P("fsdp", None),
        P("fsdp"),
        P("fsdp", None),
        P("fsdp"),
    )
    return jax.shard_map(
        per_device, mesh=mesh, in_specs=in_specs, out_specs=out_specs, check_vma=False
    )
```

profile of v0, /device:TPU:0, one launch (start us, length us, event | category | flops | bytes accessed | tf_op | source)
XLA Modules:
  0.0 1121.6 jit_solution(8430259839319301549)
XLA Ops:
  10.1 23.6 %all-gather = bf16[16,64,2]{1,2,0:T(2,128)(2,1)S(1)} all-gather(bf16[1,64,2]{1,2,0:T(2,128)(2,1)} %bitcast.245), channel_id=1, replica_groups=mesh['seq'=2,'fsdp'=16] {'fsdp'}, dimensions={0}, use_global_device_ids=true | all-gather | bytes 4352 | tf_op jit(solution)/shard_map/all_gather | solution.py:102
  38.8 59.6 %all-reduce.14 = (bf16[1024]{0:T(1024)(128)(2,1)S(1)}, bf16[1024]{0:T(1024)(128)(2,1)S(1)}, bf16[1024]{0:T(1024)(128)(2,1)S(1)}, bf16[1024]{0:T(1024)(128)(2,1)}...) all-reduce(bf16[1024]{0:T(1024)(128)(2,1)S(1)} %dynamic-update-slic, ...), channel_id=1, replica_groups=mesh['seq'=2,'fsdp'=16] {'fsdp'}, use_global_device_ids=true, to_apply=%add.1 | all-reduce | flops 6144 | bytes 24576
  98.5 8.1 add_convert_fusion
  106.7 8.3 reshape.247
  115.0 8.6 copy.73
  123.6 5.5 all-to-all-start
  129.2 31.7 %all-to-all-done = bf16[512,3,2,512]{0,3,1,2:T(8,128)(2,1)} async-done(((bf16[512,3,2,512]{0,3,1,2:T(8,128)(2,1)}), bf16[512,3,2,512]{0,3,1,2:T(8,128)(2,1)}, u32[]{:S(2)}, u32[]{:S(2)}) %all-to-all-start) | async-done | bytes 3145760 | tf_op jit(solution)/shard_map/all_to_all | solution.py:114
  160.9 6.8 copy.74
  167.7 6.1 reshape.248
  173.8 3.3 slice_bitcast_fusion
  178.9 1.8 copy.76
  180.6 2.0 copy.77
  182.7 47.9 %while.24 = (s32[]{:T(128)}, bf16[8,1024,64]{1,2,0:T(8,128)(2,1)}, f32[8,1024]{1,0:T(8,128)S(1)}, bf16[8,1024,64]{2,1,0:T(8,128)(2,1)}, bf16[8,1024,64]{2,1,0:T(...) while((s32[]{:T(128)}, bf16[8,1024,64]{1,2,0:T(8,128)(2,1)}, ...), condition=%wide.region_5.6_spmd.clone, body=%wide.region_2.5_spmd.clone.sunk | while | flops 282131456 | bytes 13548157 | solution.py:53
  183.3 3.2 fusion.152
  189.3 3.2 fusion.152
  195.2 3.2 fusion.152
  201.2 3.3 fusion.152
  207.3 3.2 fusion.152
  213.3 3.2 fusion.152
  219.2 3.2 fusion.152
  225.2 3.2 fusion.152
  231.2 3.4 reduce.7
  234.6 2.3 copy.99
  236.9 2.6 reshape.301
  239.5 4.4 all-to-all-start.1
  244.0 19.0 %all-gather.1 = bf16[16,1,256]{2,1,0:T(2,128)(2,1)S(1)} all-gather(bf16[1,1,256]{2,1,0:T(2,128)(2,1)S(1)} %reshape.275), channel_id=1, replica_groups=mesh['seq'=2,'fsdp'=16] {'fsdp'}, dimensions={0}, use_global_device_ids=true | all-gather | bytes 8704 | tf_op jit(solution)/shard_map/all_gather | solution.py:132
  263.0 2.0 reshape.302
  266.2 2.4 copy.79
  268.6 3.3 fusion.115
  272.3 10.6 fusion.109
  282.9 14.3 %convert_reduce_fusion = (f32[4096]{0:T(1024)}, bf16[512,4096]{1,0:T(8,128)(2,1)S(1)}) fusion(f32[512,4096]{1,0:T(8,128)} %fusion.109, f32[4096]{0:T(1024)S(1)} %bitcast.240, bf16[4096,1024]{1,0:T(8,128)(2,1)} %all-gather.13.cloned.1.call-done, bf16[1,512,1024]{2,1,0:T(8,128)(2,1)S(1)} %copy-done.6), kind=kOutput, calls=%fused_computation.72 | convolution fusion | flops 4343197696 | bytes 22052864 | tf_op jit(solution)/shard_map/dot_general | solution.py:32
  297.2 5.0 multiply_reduce_fusion.1
  307.9 3.6 all-to-all-start.2
  311.6 3.3 fusion.116
  315.0 10.9 all-to-all-done.2
  327.9 99.5 %while.25 = (s32[]{:T(128)}, bf16[8,3,1024,64]{2,3,0,1:T(8,128)(2,1)}, bf16[8,1024,64]{2,1,0:T(8,128)(2,1)}, bf16[8,1024,64]{2,1,0:T(8,128)(2,1)}, f32[8]{0:T(12...) while((s32[]{:T(128)}, ...), condition=%wide.region_12.13_spmd.clone, body=%wide.region_10.12_spmd.clone.sunk | while | flops 688323584 | bytes 34241164 | solution.py:71
  330.1 4.3 multiply_reduce_fusion.5
  342.6 4.3 multiply_reduce_fusion.5
  355.0 4.3 multiply_reduce_fusion.5
  367.5 4.3 multiply_reduce_fusion.5
  379.9 4.3 multiply_reduce_fusion.5
  392.3 4.3 multiply_reduce_fusion.5
  404.7 4.3 multiply_reduce_fusion.5
  417.1 4.3 multiply_reduce_fusion.5
  427.3 7.6 copy.87
  434.9 51.4 %all_to_all.60 = bf16[1024,3,1,512]{3,1,2,0:T(4,128)(2,1)S(1)} all-to-all(bf16[1024,3,1,512]{3,1,2,0:T(4,128)(2,1)} %copy.87), channel_id=1, replica_groups=mesh['seq'=2,'fsdp'=16] {'seq'}, dimensions={0} | all-to-all | bytes 6291456 | tf_op jit(solution)/shard_map/all_to_all | solution.py:175
  487.1 2.8 copy.89
  490.0 10.5 fusion.88
  500.8 16.2 %fusion.108 = f32[1024,4096]{1,0:T(8,128)} fusion(bf16[512,4096]{1,0:T(8,128)(2,1)} %copy-done.33, f32[512,1024]{1,0:T(8,128)} %copy-done.4, f32[1024]{0:T(1024)S(1)} %convert_element_type.192, f32[1024]{0:T(1024)S(1)} %convert_element_type.191, f32[512]{0:T(512)S(1)} %fusion.106, f32[512]{0:T(512)S(1)} %broadcast_multiply_fusion), kind=kOutput, calls=%fused_computation.153 | convolution fusion | flops 4297588736 | bytes 23080960 | tf_op jit(solution)/shard_map/dot_general | solution.py:26
  517.1 17.9 %fusion.91 = f32[4096,1024]{1,0:T(8,128)} fusion(bf16[1,512,1024]{2,1,0:T(8,128)(2,1)} %param.33, f32[512,4096]{1,0:T(8,128)} %fusion.109, f32[4096]{0:T(1024)S(1)} %bitcast.241), kind=kOutput, calls=%fused_computation.116 | convolution fusion | flops 4315938816 | bytes 26230784 | tf_op jit(solution)/shard_map/dot_general | solution.py:26
  538.8 12.9 %fusion.85 = bf16[1,512,1024]{2,1,0:T(8,128)(2,1)} fusion(f32[512,1024]{1,0:T(8,128)} %copy-done.4, bf16[4096,1024]{1,0:T(8,128)(2,1)} %all-gather.13.cloned.1.call-done, f32[1024]{0:T(1024)S(1)} %convert_element_type.196, f32[512,4096]{1,0:T(8,128)} %fusion.109, f32[4096]{0:T(1024)S(1)} %bitcast.242), kind=kOutput, calls=%fused_computation.109 | convolution fusion | flops 4317511680 | bytes 19943424 | tf_op jit(solution)/shard_map/dot_general | solution.py:22
  553.4 79.2 %reduce-scatter.8.cloned.1.call-done = f32[64,3072]{1,0:T(8,128)} async-done(((f32[1024,3072]{1,0:T(8,128)}), f32[64,3072]{1,0:T(8,128)}) %reduce-scatter.8.cloned.1.call-update) | async-done | bytes 786448 | tf_op jit(solution)/shard_map/reduce_scatter | solution.py:188
  632.6 1.9 convert_element_type.208
  634.5 178.8 %reduce-scatter.12.cloned.1.call-done = f32[64,4096]{1,0:T(8,128)} async-done(((f32[1024,4096]{1,0:T(8,128)}), f32[64,4096]{1,0:T(8,128)}) %reduce-scatter.12.cloned.1.call-update) | async-done | bytes 1048592 | tf_op jit(solution)/shard_map/reduce_scatter | solution.py:194
  813.4 2.1 convert_element_type.222
  815.4 178.5 %reduce-scatter.14.cloned.1.call-done = f32[256,1024]{1,0:T(8,128)} async-done(((f32[4096,1024]{1,0:T(8,128)}), f32[256,1024]{1,0:T(8,128)}) %reduce-scatter.14.cloned.1.call-update) | async-done | bytes 1048592 | tf_op jit(solution)/shard_map/reduce_scatter | solution.py:196
  993.9 2.1 convert_element_type.227
  996.1 6.9 fusion.110
  1004.8 2.1 convert_reduce_fusion.3
  1007.0 59.6 %all-reduce.13 = (bf16[1024]{0:T(1024)(128)(2,1)S(1)}, bf16[1024]{0:T(1024)(128)(2,1)S(1)}, bf16[1024]{0:T(1024)(128)(2,1)S(1)}, bf16[1024]{0:T(1024)(128)(2,1)S...) all-reduce(f32[1024]{0:T(1024)S(1)} %get-tuple-element.229, ...), channel_id=2, replica_groups=mesh['seq'=2,'fsdp'=16] {'fsdp'}, use_global_device_ids=true, to_apply=%region_16.17.clone | all-reduce | flops 10240 | bytes 61440
  1068.0 5.1 all-reduce.15
  1077.3 30.3 %all-reduce.19.cloned.1.call-done = (bf16[64,3072]{1,0:T(8,128)(2,1)}, bf16[64,1024]{1,0:T(8,128)(2,1)}, bf16[64,4096]{1,0:T(8,128)(2,1)}, bf16[256,1024]{1,0:T(8,128)(2,1)}) async-done(((bf16[64,3072]{1,0:T(8,128)(2,1)}, bf16[64,1024]{1,0:T(8,128)(2,1)}, bf16[64,4096]{1,0:T(8,128)(2,1)}, bf16[256,1024]{1,0:T(8,128)(2,1)}), (bf16[64,3072]{1,0:T(8,128)(2,1)}, bf16[64,1024]{1,0:T(8,128)(2,1)}, ...) | async-done | bytes 1572880 | tf_op jit(solution)/shard_map/psum | solution.py:204
  1107.6 2.0 convert_element_type.209
  1111.2 2.1 convert_element_type.223
  (276 shorter events, 121.5 us)
Async XLA Ops:
  7.2 29.0 %copy-start.23 = (u32[32]{0:T(128)S(1)}, u32[32]{0:T(128)}, u32[]{:S(2)}) copy-start(u32[32]{0:T(128)} %constant.97) | copy-start | bytes 388
  7.2 28.0 %copy-start = (bf16[1,512,1024]{2,1,0:T(8,128)(2,1)S(1)}, bf16[1,512,1024]{2,1,0:T(8,128)(2,1)}, u32[]{:S(2)}) copy-start(bf16[1,512,1024]{2,1,0:T(8,128)(2,1)} %param.19) | copy-start | bytes 3145732
  7.2 30.2 %copy-start.26 = (bf16[64]{0:T(256)(128)(2,1)S(1)}, bf16[64]{0:T(256)(128)(2,1)}, u32[]{:S(2)}) copy-start(bf16[64]{0:T(256)(128)(2,1)} %param.22) | copy-start | bytes 388
  7.2 30.5 %copy-start.27 = (bf16[64]{0:T(256)(128)(2,1)S(1)}, bf16[64]{0:T(256)(128)(2,1)}, u32[]{:S(2)}) copy-start(bf16[64]{0:T(256)(128)(2,1)} %param.21) | copy-start | bytes 388
  7.2 30.7 %copy-start.28 = (bf16[64]{0:T(256)(128)(2,1)S(1)}, bf16[64]{0:T(256)(128)(2,1)}, u32[]{:S(2)}) copy-start(bf16[64]{0:T(256)(128)(2,1)} %param.26) | copy-start | bytes 388
  7.2 30.9 %copy-start.29 = (bf16[64]{0:T(256)(128)(2,1)S(1)}, bf16[64]{0:T(256)(128)(2,1)}, u32[]{:S(2)}) copy-start(bf16[64]{0:T(256)(128)(2,1)} %param.32) | copy-start | bytes 388
  7.2 31.1 %copy-start.30 = (bf16[64]{0:T(256)(128)(2,1)S(1)}, bf16[64]{0:T(256)(128)(2,1)}, u32[]{:S(2)}) copy-start(bf16[64]{0:T(256)(128)(2,1)} %param.28) | copy-start | bytes 388
  7.3 31.4 %copy-start.31 = (bf16[64]{0:T(256)(128)(2,1)S(1)}, bf16[64]{0:T(256)(128)(2,1)}, u32[]{:S(2)}) copy-start(bf16[64]{0:T(256)(128)(2,1)} %param.27) | copy-start | bytes 388
  7.3 91.3 %all-gather.7.cloned.1.call-start = ((), (), s32[]{:S(2)}) async-start(), calls=%async_computation.9 | async-start | bytes 6684672 | tf_op jit(solution)/shard_map/all_gather | solution.py:101
  8.0 260.6 %all-gather.9.cloned.1.call-start = ((), (), s32[]{:S(2)}) async-start(), calls=%async_computation.10 | async-start | bytes 2228224 | tf_op jit(solution)/shard_map/all_gather | solution.py:103
  8.7 263.5 %all-gather.11.cloned.1.call-start = ((), (), s32[]{:S(2)}) async-start(), calls=%async_computation.11 | async-start | bytes 8912896 | tf_op jit(solution)/shard_map/all_gather | solution.py:131
  9.5 273.4 %all-gather.13.cloned.1.call-start = ((), (), s32[]{:S(2)}) async-start(), calls=%async_computation.12 | async-start | bytes 8912896 | tf_op jit(solution)/shard_map/all_gather | solution.py:133
  35.2 71.5 %copy-start.13 = (f32[512]{0:T(512)}, f32[512]{0:T(512)S(1)}, u32[]{:S(2)}) copy-start(f32[512]{0:T(512)S(1)} %broadcast_multiply_fusion.1) | copy-start | bytes 6148
  35.6 0.6 copy-start.17
  35.6 71.1 %copy-start.15 = (f32[512]{0:T(512)}, f32[512]{0:T(512)S(1)}, u32[]{:S(2)}) copy-start(f32[512]{0:T(512)S(1)} %fusion.105) | copy-start | bytes 6148
  98.5 8.2 copy-start.20
  98.5 8.2 copy-start.11
  123.6 37.3 %all-to-all-start = ((bf16[512,3,2,512]{0,3,1,2:T(8,128)(2,1)}), bf16[512,3,2,512]{0,3,1,2:T(8,128)(2,1)}, u32[]{:S(2)}, u32[]{:S(2)}) async-start(bf16[512,3,2,512]{0,3,1,2:T(8,128)(2,1)} %copy.73), calls=%async_computation | async-start | bytes 6291456 | tf_op jit(solution)/shard_map/all_to_all | solution.py:114
  178.9 3.8 copy-start.25
  230.6 8.9 copy-start.5
  234.6 9.4 copy-start.32
  239.5 23.5 %all-to-all-start.1 = ((bf16[2,2,131072]{2,1,0:T(2,128)(2,1)}), bf16[2,2,131072]{2,1,0:T(2,128)(2,1)}, u32[]{:S(2)}, u32[]{:S(2)}) async-start(bf16[2,2,131072]{2,1,0:T(2,128)(2,1)} %reshape.301), calls=%async_computation.1 | async-start | bytes 2097152 | tf_op jit(solution)/shard_map/all_to_all | solution.py:124
  271.8 30.4 %copy-start.4 = (f32[512,1024]{1,0:T(8,128)}, f32[512,1024]{1,0:T(8,128)S(1)}, u32[]{:S(2)}) copy-start(f32[512,1024]{1,0:T(8,128)S(1)} %get-tuple-element.313) | copy-start | bytes 6291460
  272.2 10.7 copy-start.6
  282.9 14.3 %copy-start.24 = (bf16[1024,4096]{1,0:T(8,128)(2,1)S(1)}, bf16[1024,4096]{1,0:T(8,128)(2,1)}, u32[]{:S(2)}) copy-start(bf16[1024,4096]{1,0:T(8,128)(2,1)} %all-gather.11.cloned.1.call-done) | copy-start | bytes 25165828
  297.2 5.0 copy-start.33
  302.9 1.3 copy-start.2
  302.9 2.4 copy-start.9
  306.6 5.0 copy-start.8
  307.9 17.9 %all-to-all-start.2 = ((bf16[512,2,512]{0,2,1:T(8,128)(2,1)}), bf16[512,2,512]{0,2,1:T(8,128)(2,1)S(1)}, u32[]{:S(2)}, u32[]{:S(2)}) async-start(bf16[512,2,512]{0,2,1:T(8,128)(2,1)} %bitcast.19), calls=%async_computation.2 | async-start | bytes 2097152 | tf_op jit(solution)/shard_map/all_to_all | solution.py:171
  311.5 240.2 %reduce-scatter.10.cloned.1.call-start = ((), (), s32[]{:S(2)}) async-start(), calls=%async_computation.14 | async-start | bytes 4456448 | tf_op jit(solution)/shard_map/reduce_scatter | solution.py:190
  314.9 317.7 %reduce-scatter.8.cloned.1.call-start = ((), (), s32[]{:S(2)}) async-start(), calls=%async_computation.13 | async-start | bytes 13369344 | tf_op jit(solution)/shard_map/reduce_scatter | solution.py:188
  487.1 2.9 copy-start.12
  487.1 2.9 copy-start.14
  487.1 2.9 copy-start.16
  487.1 2.9 copy-start.21
  500.5 312.8 %reduce-scatter.12.cloned.1.call-start = ((), (), s32[]{:S(2)}) async-start(), calls=%async_computation.15 | async-start | bytes 17825792 | tf_op jit(solution)/shard_map/reduce_scatter | solution.py:194
  517.0 476.9 %reduce-scatter.14.cloned.1.call-start = ((), (), s32[]{:S(2)}) async-start(), calls=%async_computation.16 | async-start | bytes 17825792 | tf_op jit(solution)/shard_map/reduce_scatter | solution.py:196
  535.0 0.7 copy-start.22
  535.0 532.1 %reduce-scatter.16.cloned.1.call-start = ((), (), s32[]{:S(2)}) async-start(), calls=%async_computation.17 | async-start | bytes 557056
  538.5 569.1 %all-reduce.19.cloned.1.call-start = ((), (), s32[]{:S(2)}) async-start(), calls=%async_computation.18 | async-start | bytes 3145728 | tf_op jit(solution)/shard_map/psum | solution.py:204
  551.7 444.4 %copy-start.1 = (bf16[1,512,1024]{2,1,0:T(8,128)(2,1)S(1)}, bf16[1,512,1024]{2,1,0:T(8,128)(2,1)}, u32[]{:S(2)}) copy-start(bf16[1,512,1024]{2,1,0:T(8,128)(2,1)} %param.19) | copy-start | bytes 3145732
  996.1 6.9 copy-start.18
  1003.0 1.6 copy-start.3
  1003.0 1.9 copy-start.7
  1004.8 2.1 copy-start.19
  1107.6 5.7 copy-start.10
Sparse Core Ops, SparseCore 0:
  10.4 64.7 all-gather.6
  77.3 40.1 all-gather.8
  119.6 72.9 all-gather.10
  194.7 72.9 all-gather.12
  315.8 70.6 reduce-scatter.9
  500.7 131.9 reduce-scatter.7
  636.7 176.6 reduce-scatter.11
  817.5 176.4 reduce-scatter.13
  998.1 55.2 reduce-scatter.15
  1056.8 50.7 all-reduce.18
where the time goes:
time: 1130 us; the launch traced here: 1120 us
  waiting for transfers between devices  512 us (45%)
  matrix products  227 us (20%)
  blocking collectives  218 us (19%)
  local copies, waits for them, and re-layouts  82.9 us (7%)
  other arithmetic  49.6 us (4%)
  between operations  17.2 us (2%)
  starting transfers between devices  14.4 us (1%)
    reduce_scatter x1, waiting for transfers between devices, per_device(): lax.psum_scatter(grad_up_weight, 'fsdp', scatter_dimension=0, tiled=True)  179 us
    reduce_scatter x1, waiting for transfers between devices, per_device(): lax.psum_scatter(grad_down_weight, 'fsdp', scatter_dimension=0, tiled=True)  178 us
    unnamed x2, blocking collectives  119 us
    dot_general x28, matrix products, right_contract(): lax.dot_general(left, right, (((1,), (1,)), ((), ())), preferred_element_...  100 us
    reduce_scatter x1, waiting for transfers between devices, per_device(): lax.psum_scatter(grad_joint_weight, 'fsdp', scatter_dimension=0, tiled=True)  79.2 us
    dot_general x20, matrix products, left_contract(): lax.dot_general(left, right, (((0,), (0,)), ((), ())), preferred_element_...  67.8 us
    dot_general x20, matrix products, matmul(): return jnp.dot(left, right, preferred_element_type=jnp.float32)  58.5 us
    all_to_all x1, blocking collectives, per_device(): lax.all_to_all(grad_stack, 'seq', split_axis=0, concat_axis=2, tiled=True)  51.4 us
  transfers between devices with their start and end apart: 13, of which 6 were waited for; matrix products, arithmetic and copies ran while one was open for 29% of the time, Pallas kernels for 0%

commit v1 on v0

--- a/solution.py
+++ b/solution.py
@@ -201,7 +201,9 @@
     totals = (
         lax.psum(attn_sums[0].astype(jnp.bfloat16), "seq").astype(jnp.float32),
         lax.psum(attn_sums[1].astype(jnp.bfloat16), "seq").astype(jnp.float32),
-        lax.psum(attn_sums[2].astype(jnp.bfloat16), "seq").astype(jnp.float32),
+        jnp.sum(lax.all_gather(attn_sums[2].astype(jnp.bfloat16), "seq"), axis=0).astype(
+            jnp.float32
+        ),
         lax.psum(attn_sums[3].astype(jnp.bfloat16), "seq").astype(jnp.float32),
         lax.psum(attn_sums[4].astype(jnp.bfloat16), "seq").astype(jnp.float32),
         lax.psum(attn_sums[5].astype(jnp.bfloat16), "seq").astype(jnp.float32),

time: 1130 us -> 1010 us (0.89)
  waiting for transfers between devices: 512 us -> 377 us
  blocking collectives: 218 us -> 233 us
    reduce_scatter x1, waiting for transfers between devices: 179 us -> 0.01 us  [per_device(): lax.psum_scatter(grad_up_weight, 'fsdp', scatter_dimension=0, tiled=True)]
    reduce_scatter x1, waiting for transfers between devices: 79.2 us -> 121 us  [per_device(): lax.psum_scatter(grad_joint_weight, 'fsdp', scatter_dimension=0, tiled=True)]
    all_gather x0 -> x1, blocking collectives: none -> 14.6 us  [per_device(): lax.all_gather(attn_sums[2].astype(jnp.bfloat16), 'seq')]
    unnamed x103 -> x111, local copies, waits for them, and re-layouts: 22.1 us -> 23.4 us
  transfers between devices with their start and end apart: 13 -> 13, of which waited for: 6 -> 5; matrix products, arithmetic and copies ran while one was open for 29% -> 32% of each run, Pallas kernels for 0% -> 0%
where the time goes in v1:
time: 1010 us; the launch traced here: 999 us
  waiting for transfers between devices  377 us (37%)
  blocking collectives  233 us (23%)
  matrix products  222 us (22%)
  local copies, waits for them, and re-layouts  84.9 us (8%)
  other arithmetic  50.7 us (5%)
  between operations  17.2 us (2%)
  starting transfers between devices  14.6 us (1%)
    reduce_scatter x1, waiting for transfers between devices, per_device(): lax.psum_scatter(grad_down_weight, 'fsdp', scatter_dimension=0, tiled=True)  177 us
    reduce_scatter x1, waiting for transfers between devices, per_device(): lax.psum_scatter(grad_joint_weight, 'fsdp', scatter_dimension=0, tiled=True)  121 us
    unnamed x2, blocking collectives  119 us
    dot_general x28, matrix products, right_contract(): lax.dot_general(left, right, (((1,), (1,)), ((), ())), preferred_element_...  103 us
    dot_general x20, matrix products, left_contract(): lax.dot_general(left, right, (((0,), (0,)), ((), ())), preferred_element_...  60.8 us
    dot_general x20, matrix products, matmul(): return jnp.dot(left, right, preferred_element_type=jnp.float32)  58.2 us
    all_to_all x1, blocking collectives, per_device(): lax.all_to_all(grad_stack, 'seq', split_axis=0, concat_axis=2, tiled=True)  51.3 us
    all_to_all x1, waiting for transfers between devices, per_device(): lax.all_to_all(joint, 'seq', split_axis=2, concat_axis=0, tiled=True)  31.7 us
  transfers between devices with their start and end apart: 13, of which 5 were waited for; matrix products, arithmetic and copies ran while one was open for 32% of the time, Pallas kernels for 0%

profile of v1, /device:TPU:0, one launch (start us, length us, event | category | flops | bytes accessed | tf_op | source)
XLA Modules:
  0.0 999.4 jit_solution(13422148159150170370)
XLA Ops:
  10.1 23.6 %all-gather.1 = bf16[16,64,2]{1,2,0:T(2,128)(2,1)S(1)} all-gather(bf16[1,64,2]{1,2,0:T(2,128)(2,1)} %bitcast.247), channel_id=1, replica_groups=mesh['seq'=2,'fsdp'=16] {'fsdp'}, dimensions={0}, use_global_device_ids=true | all-gather | bytes 4352 | tf_op jit(solution)/shard_map/all_gather | solution.py:102
  38.8 59.6 %all-reduce.14 = (bf16[1024]{0:T(1024)(128)(2,1)S(1)}, bf16[1024]{0:T(1024)(128)(2,1)S(1)}, bf16[1024]{0:T(1024)(128)(2,1)S(1)}, bf16[1024]{0:T(1024)(128)(2,1)}...) all-reduce(bf16[1024]{0:T(1024)(128)(2,1)S(1)} %dynamic-update-slic, ...), channel_id=1, replica_groups=mesh['seq'=2,'fsdp'=16] {'fsdp'}, use_global_device_ids=true, to_apply=%add.1 | all-reduce | flops 6144 | bytes 24576
  98.5 8.1 add_convert_fusion
  106.7 8.3 reshape.247
  115.0 8.6 copy.73
  123.6 5.5 all-to-all-start
  129.2 31.7 %all-to-all-done = bf16[512,3,2,512]{0,3,1,2:T(8,128)(2,1)} async-done(((bf16[512,3,2,512]{0,3,1,2:T(8,128)(2,1)}), bf16[512,3,2,512]{0,3,1,2:T(8,128)(2,1)}, u32[]{:S(2)}, u32[]{:S(2)}) %all-to-all-start) | async-done | bytes 3145760 | tf_op jit(solution)/shard_map/all_to_all | solution.py:114
  160.9 6.8 copy.74
  167.7 6.1 reshape.248
  173.8 3.3 slice_bitcast_fusion
  180.7 2.0 copy.77
  182.7 47.9 %while.24 = (s32[]{:T(128)}, bf16[8,1024,64]{1,2,0:T(8,128)(2,1)}, f32[8,1024]{1,0:T(8,128)S(1)}, bf16[8,1024,64]{2,1,0:T(8,128)(2,1)}, bf16[8,1024,64]{2,1,0:T(...) while((s32[]{:T(128)}, bf16[8,1024,64]{1,2,0:T(8,128)(2,1)}, ...), condition=%wide.region_5.6_spmd.clone, body=%wide.region_2.5_spmd.clone.sunk | while | flops 282131456 | bytes 13548157 | solution.py:53
  183.3 3.2 fusion.152
  189.3 3.2 fusion.152
  195.3 3.2 fusion.152
  201.2 3.3 fusion.152
  207.3 3.2 fusion.152
  213.3 3.2 fusion.152
  219.3 3.2 fusion.152
  225.2 3.2 fusion.152
  231.2 3.4 reduce.8
  234.6 2.3 copy.100
  236.8 2.6 reshape.302
  239.5 4.4 all-to-all-start.1
  244.0 19.0 %all-gather.2 = bf16[16,1,256]{2,1,0:T(2,128)(2,1)S(1)} all-gather(bf16[1,1,256]{2,1,0:T(2,128)(2,1)S(1)} %reshape.276), channel_id=1, replica_groups=mesh['seq'=2,'fsdp'=16] {'fsdp'}, dimensions={0}, use_global_device_ids=true | all-gather | bytes 8704 | tf_op jit(solution)/shard_map/all_gather | solution.py:132
  266.3 2.3 copy.79
  268.6 3.3 fusion.115
  272.3 10.6 %fusion.109 = f32[512,4096]{1,0:T(8,128)} fusion(bf16[1024,4096]{1,0:T(8,128)(2,1)} %all-gather.12.cloned.1.call-done, f32[512,1024]{1,0:T(8,128)S(1)} %get-tuple-element.312, f32[1024]{0:T(1024)S(1)} %convert_element_type.194, f32[1024]{0:T(1024)S(1)} %convert_element_type.193, f32[512]{0:T(512)S(1)} %fusion.106, f32[512]{0:T(512)S(1)} %broadcast_multiply_fusion), kind=kOutput, calls=%fused_computation.154 | convolution fusion | flops 4297588736 | bytes 18886656 | tf_op jit(solution)/shard_map/dot_general | solution.py:22
  283.0 14.3 %convert_reduce_fusion = (f32[4096]{0:T(1024)}, bf16[512,4096]{1,0:T(8,128)(2,1)S(1)}) fusion(f32[512,4096]{1,0:T(8,128)} %fusion.109, f32[4096]{0:T(1024)S(1)} %bitcast.242, bf16[4096,1024]{1,0:T(8,128)(2,1)} %all-gather.14.cloned.1.call-done, bf16[1,512,1024]{2,1,0:T(8,128)(2,1)S(1)} %copy-done.8), kind=kOutput, calls=%fused_computation.72 | convolution fusion | flops 4343197696 | bytes 22052864 | tf_op jit(solution)/shard_map/dot_general | solution.py:32
  297.3 5.0 multiply_reduce_fusion.1
  305.6 3.3 fusion.116
  309.0 11.0 %fusion.108 = f32[1024,4096]{1,0:T(8,128)} fusion(bf16[512,4096]{1,0:T(8,128)(2,1)} %copy-done.37, f32[512,1024]{1,0:T(8,128)S(1)} %get-tuple-element.312, f32[1024]{0:T(1024)S(1)} %convert_element_type.194, f32[1024]{0:T(1024)S(1)} %convert_element_type.193, f32[512]{0:T(512)S(1)} %fusion.106, f32[512]{0:T(512)S(1)} %broadcast_multiply_fusion), kind=kOutput, calls=%fused_computation.153 | convolution fusion | flops 4297588736 | bytes 23080960 | tf_op jit(solution)/shard_map/dot_general | solution.py:26
  320.2 16.1 %fusion.91 = f32[4096,1024]{1,0:T(8,128)} fusion(bf16[1,512,1024]{2,1,0:T(8,128)(2,1)S(1)} %copy-done.8, f32[512,4096]{1,0:T(8,128)} %fusion.109, f32[4096]{0:T(1024)S(1)} %bitcast.243), kind=kOutput, calls=%fused_computation.116 | convolution fusion | flops 4315938816 | bytes 26230784 | tf_op jit(solution)/shard_map/dot_general | solution.py:26
  338.3 2.3 convolution_convert_fusion
  340.6 2.3 copy.90
  342.8 3.6 all-to-all-start.2
  346.7 14.1 %all-to-all-done.2 = bf16[512,2,512]{0,2,1:T(8,128)(2,1)S(1)} async-done(((bf16[512,2,512]{0,2,1:T(8,128)(2,1)}), bf16[512,2,512]{0,2,1:T(8,128)(2,1)S(1)}, u32[]{:S(2)}, u32[]{:S(2)}) %all-to-all-start.2) | async-done | bytes 1048608 | tf_op jit(solution)/shard_map/all_to_all | solution.py:171
  362.6 99.9 %while.25 = (s32[]{:T(128)}, bf16[8,3,1024,64]{2,3,0,1:T(8,128)(2,1)}, bf16[8,1024,64]{2,1,0:T(8,128)(2,1)}, bf16[8,1024,64]{2,1,0:T(8,128)(2,1)}, f32[8]{0:T(12...) while((s32[]{:T(128)}, ...), condition=%wide.region_12.13_spmd.clone, body=%wide.region_10.12_spmd.clone.sunk | while | flops 688323584 | bytes 34241164 | solution.py:71
  364.9 4.3 multiply_reduce_fusion.5
  377.3 4.3 multiply_reduce_fusion.5
  389.8 4.4 multiply_reduce_fusion.5
  402.5 4.3 multiply_reduce_fusion.5
  415.0 4.3 multiply_reduce_fusion.5
  427.4 4.3 multiply_reduce_fusion.5
  439.8 4.3 multiply_reduce_fusion.5
  452.3 4.3 multiply_reduce_fusion.5
  462.5 7.6 copy.87
  470.1 51.3 %all_to_all.60 = bf16[1024,3,1,512]{3,1,2,0:T(4,128)(2,1)S(1)} all-to-all(bf16[1024,3,1,512]{3,1,2,0:T(4,128)(2,1)} %copy.87), channel_id=1, replica_groups=mesh['seq'=2,'fsdp'=16] {'seq'}, dimensions={0} | all-to-all | bytes 6291456 | tf_op jit(solution)/shard_map/all_to_all | solution.py:175
  522.2 2.8 copy.89
  526.7 10.5 %fusion.88 = f32[1024,3072]{1,0:T(8,128)} fusion(bf16[512,3072]{0,1:T(8,128)(2,1)} %bitcast.233, bf16[1,512,1024]{2,1,0:T(8,128)(2,1)} %param.19, f32[1024]{0:T(1024)S(1)} %copy-done.25, f32[1024]{0:T(1024)S(1)} %copy-done.16, f32[512]{0:T(512)S(1)} %copy-done.20, f32[512]{0:T(512)S(1)} %copy-done.18), kind=kOutput, calls=%fused_computation.112 | convolution fusion | flops 3224371200 | bytes 16789504 | tf_op jit(solution)/shard_map/dot_general | solution.py:26
  539.2 12.5 %fusion.85 = bf16[1,512,1024]{2,1,0:T(8,128)(2,1)} fusion(f32[512,1024]{1,0:T(8,128)S(1)} %copy-done.5, bf16[4096,1024]{1,0:T(8,128)(2,1)} %all-gather.14.cloned.1.call-done, f32[1024]{0:T(1024)S(1)} %convert_element_type.198, f32[512,4096]{1,0:T(8,128)} %fusion.109, f32[4096]{0:T(1024)S(1)} %bitcast.244), kind=kOutput, calls=%fused_computation.109 | convolution fusion | flops 4317511680 | bytes 19943424 | tf_op jit(solution)/shard_map/dot_general | solution.py:22
  551.8 7.9 fusion.110
  561.3 2.1 convert_element_type.224
  563.4 177.4 %reduce-scatter.14.cloned.1.call-done = f32[256,1024]{1,0:T(8,128)} async-done(((f32[4096,1024]{1,0:T(8,128)}), f32[256,1024]{1,0:T(8,128)}) %reduce-scatter.14.cloned.1.call-update) | async-done | bytes 1048592 | tf_op jit(solution)/shard_map/reduce_scatter | solution.py:196
  740.8 2.1 convert_element_type.229
  743.0 2.7 fusion.77
  745.7 2.2 convert_reduce_fusion.3
  747.9 59.6 %all-reduce.13 = (bf16[1024]{0:T(1024)(128)(2,1)S(1)}, bf16[1024]{0:T(1024)(128)(2,1)S(1)}, bf16[1024]{0:T(1024)(128)(2,1)S(1)}, bf16[1024]{0:T(1024)(128)(2,1)S...) all-reduce(f32[1024]{0:T(1024)S(1)} %get-tuple-element.229, ...), channel_id=3, replica_groups=mesh['seq'=2,'fsdp'=16] {'fsdp'}, use_global_device_ids=true, to_apply=%region_16.17.clone | all-reduce | flops 10240 | bytes 61440
  808.8 4.9 all-reduce.15
  817.9 120.5 %reduce-scatter.8.cloned.1.call-done = f32[64,3072]{1,0:T(8,128)} async-done(((f32[1024,3072]{1,0:T(8,128)}), f32[64,3072]{1,0:T(8,128)}) %reduce-scatter.8.cloned.1.call-update) | async-done | bytes 786448 | tf_op jit(solution)/shard_map/reduce_scatter | solution.py:188
  939.7 14.6 %all-gather = bf16[128,3072]{1,0:T(8,128)(2,1)S(1)} all-gather(bf16[64,3072]{1,0:T(8,128)(2,1)S(1)} %convert_element_type.210), channel_id=2, replica_groups=mesh['seq'=2,'fsdp'=16] {'seq'}, dimensions={0}, use_global_device_ids=true | all-gather | bytes 1179648 | tf_op jit(solution)/shard_map/all_gather | solution.py:204
  955.5 30.8 %all-reduce.19.cloned.1.call-done = (bf16[64,1024]{1,0:T(8,128)(2,1)}, bf16[64,4096]{1,0:T(8,128)(2,1)}, bf16[256,1024]{1,0:T(8,128)(2,1)}) async-done(((bf16[64,1024]{1,0:T(8,128)(2,1)}, bf16[64,4096]{1,0:T(8,128)(2,1)}, bf16[256,1024]{1,0:T(8,128)(2,1)}), (bf16[64,1024]{1,0:T(8,128)(2,1)}, bf16[64,4096]{1,0:T(8,128)(2,1)}, bf16[256,1024]{1,0:T(8,128)(2,1)})) %all-reduce.19.cloned.1.call-update) | async-done | bytes 1179664 | tf_op jit(solution)/shard_map/psum | solution.py:208
  987.9 2.1 convert_element_type.225
  990.0 2.1 convert_element_type.230
  (286 shorter events, 124.4 us)
Async XLA Ops:
  7.2 29.0 %copy-start.27 = (u32[32]{0:T(128)S(1)}, u32[32]{0:T(128)}, u32[]{:S(2)}) copy-start(u32[32]{0:T(128)} %constant.98) | copy-start | bytes 388
  7.2 28.0 %copy-start = (bf16[1,512,1024]{2,1,0:T(8,128)(2,1)S(1)}, bf16[1,512,1024]{2,1,0:T(8,128)(2,1)}, u32[]{:S(2)}) copy-start(bf16[1,512,1024]{2,1,0:T(8,128)(2,1)} %param.19) | copy-start | bytes 3145732
  7.2 30.2 %copy-start.30 = (bf16[64]{0:T(256)(128)(2,1)S(1)}, bf16[64]{0:T(256)(128)(2,1)}, u32[]{:S(2)}) copy-start(bf16[64]{0:T(256)(128)(2,1)} %param.22) | copy-start | bytes 388
  7.2 30.5 %copy-start.31 = (bf16[64]{0:T(256)(128)(2,1)S(1)}, bf16[64]{0:T(256)(128)(2,1)}, u32[]{:S(2)}) copy-start(bf16[64]{0:T(256)(128)(2,1)} %param.21) | copy-start | bytes 388
  7.2 30.7 %copy-start.32 = (bf16[64]{0:T(256)(128)(2,1)S(1)}, bf16[64]{0:T(256)(128)(2,1)}, u32[]{:S(2)}) copy-start(bf16[64]{0:T(256)(128)(2,1)} %param.26) | copy-start | bytes 388
  7.2 30.9 %copy-start.33 = (bf16[64]{0:T(256)(128)(2,1)S(1)}, bf16[64]{0:T(256)(128)(2,1)}, u32[]{:S(2)}) copy-start(bf16[64]{0:T(256)(128)(2,1)} %param.32) | copy-start | bytes 388
  7.2 31.1 %copy-start.34 = (bf16[64]{0:T(256)(128)(2,1)S(1)}, bf16[64]{0:T(256)(128)(2,1)}, u32[]{:S(2)}) copy-start(bf16[64]{0:T(256)(128)(2,1)} %param.28) | copy-start | bytes 388
  7.3 31.4 %copy-start.35 = (bf16[64]{0:T(256)(128)(2,1)S(1)}, bf16[64]{0:T(256)(128)(2,1)}, u32[]{:S(2)}) copy-start(bf16[64]{0:T(256)(128)(2,1)} %param.27) | copy-start | bytes 388
  7.3 91.3 %all-gather.8.cloned.1.call-start = ((), (), s32[]{:S(2)}) async-start(), calls=%async_computation.9 | async-start | bytes 6684672 | tf_op jit(solution)/shard_map/all_gather | solution.py:101
  8.0 260.6 %all-gather.10.cloned.1.call-start = ((), (), s32[]{:S(2)}) async-start(), calls=%async_computation.10 | async-start | bytes 2228224 | tf_op jit(solution)/shard_map/all_gather | solution.py:103
  8.7 263.6 %all-gather.12.cloned.1.call-start = ((), (), s32[]{:S(2)}) async-start(), calls=%async_computation.11 | async-start | bytes 8912896 | tf_op jit(solution)/shard_map/all_gather | solution.py:131
  9.5 273.5 %all-gather.14.cloned.1.call-start = ((), (), s32[]{:S(2)}) async-start(), calls=%async_computation.12 | async-start | bytes 8912896 | tf_op jit(solution)/shard_map/all_gather | solution.py:133
  35.2 71.5 %copy-start.17 = (f32[512]{0:T(512)}, f32[512]{0:T(512)S(1)}, u32[]{:S(2)}) copy-start(f32[512]{0:T(512)S(1)} %broadcast_multiply_fusion.1) | copy-start | bytes 6148
  35.6 0.6 copy-start.21
  35.6 71.1 %copy-start.19 = (f32[512]{0:T(512)}, f32[512]{0:T(512)S(1)}, u32[]{:S(2)}) copy-start(f32[512]{0:T(512)S(1)} %fusion.105) | copy-start | bytes 6148
  98.5 8.2 copy-start.24
  98.5 8.2 copy-start.15
  123.6 37.3 %all-to-all-start = ((bf16[512,3,2,512]{0,3,1,2:T(8,128)(2,1)}), bf16[512,3,2,512]{0,3,1,2:T(8,128)(2,1)}, u32[]{:S(2)}, u32[]{:S(2)}) async-start(bf16[512,3,2,512]{0,3,1,2:T(8,128)(2,1)} %copy.73), calls=%async_computation | async-start | bytes 6291456 | tf_op jit(solution)/shard_map/all_to_all | solution.py:114
  178.9 3.8 copy-start.29
  230.6 8.9 copy-start.6
  234.6 9.5 copy-start.36
  239.5 23.6 %all-to-all-start.1 = ((bf16[2,2,131072]{2,1,0:T(2,128)(2,1)}), bf16[2,2,131072]{2,1,0:T(2,128)(2,1)}, u32[]{:S(2)}, u32[]{:S(2)}) async-start(bf16[2,2,131072]{2,1,0:T(2,128)(2,1)} %reshape.302), calls=%async_computation.1 | async-start | bytes 2097152 | tf_op jit(solution)/shard_map/all_to_all | solution.py:124
  243.9 315.8 %reduce-scatter.10.cloned.1.call-start = ((), (), s32[]{:S(2)}) async-start(), calls=%async_computation.14 | async-start | bytes 4456448 | tf_op jit(solution)/shard_map/reduce_scatter | solution.py:190
  271.9 37.1 %copy-start.4 = (f32[512,1024]{1,0:T(8,128)}, f32[512,1024]{1,0:T(8,128)S(1)}, u32[]{:S(2)}) copy-start(f32[512,1024]{1,0:T(8,128)S(1)} %get-tuple-element.312) | copy-start | bytes 6291460
  272.3 10.7 %copy-start.8 = (bf16[1,512,1024]{2,1,0:T(8,128)(2,1)S(1)}, bf16[1,512,1024]{2,1,0:T(8,128)(2,1)}, u32[]{:S(2)}) copy-start(bf16[1,512,1024]{2,1,0:T(8,128)(2,1)} %param.33) | copy-start | bytes 3145732
  283.0 14.3 %copy-start.28 = (bf16[1024,4096]{1,0:T(8,128)(2,1)S(1)}, bf16[1024,4096]{1,0:T(8,128)(2,1)}, u32[]{:S(2)}) copy-start(bf16[1024,4096]{1,0:T(8,128)(2,1)} %all-gather.12.cloned.1.call-done) | copy-start | bytes 25165828
  297.3 5.0 copy-start.37
  303.0 1.3 copy-start.2
  303.0 2.7 copy-start.10
  304.7 1.0 copy-start.13
  309.0 252.4 %reduce-scatter.12.cloned.1.call-start = ((), (), s32[]{:S(2)}) async-start(), calls=%async_computation.15 | async-start | bytes 17825792 | tf_op jit(solution)/shard_map/reduce_scatter | solution.py:194
  320.0 420.8 %reduce-scatter.14.cloned.1.call-start = ((), (), s32[]{:S(2)}) async-start(), calls=%async_computation.16 | async-start | bytes 17825792 | tf_op jit(solution)/shard_map/reduce_scatter | solution.py:196
  336.3 1.7 copy-start.12
  336.3 2.0 copy-start.14
  342.8 17.9 %all-to-all-start.2 = ((bf16[512,2,512]{0,2,1:T(8,128)(2,1)}), bf16[512,2,512]{0,2,1:T(8,128)(2,1)S(1)}, u32[]{:S(2)}, u32[]{:S(2)}) async-start(bf16[512,2,512]{0,2,1:T(8,128)(2,1)} %bitcast.19), calls=%async_computation.2 | async-start | bytes 2097152 | tf_op jit(solution)/shard_map/all_to_all | solution.py:171
  346.4 461.6 %reduce-scatter.16.cloned.1.call-start = ((), (), s32[]{:S(2)}) async-start(), calls=%async_computation.17 | async-start | bytes 557056
  525.0 1.6 copy-start.16
  525.0 1.6 copy-start.18
  525.0 1.6 copy-start.20
  525.0 1.6 copy-start.25
  526.6 411.9 %reduce-scatter.8.cloned.1.call-start = ((), (), s32[]{:S(2)}) async-start(), calls=%async_computation.13 | async-start | bytes 13369344 | tf_op jit(solution)/shard_map/reduce_scatter | solution.py:188
  537.2 0.7 copy-start.26
  537.2 2.0 copy-start.5
  537.2 449.1 %all-reduce.19.cloned.1.call-start = ((), (), s32[]{:S(2)}) async-start(), calls=%async_computation.18 | async-start | bytes 2359296 | tf_op jit(solution)/shard_map/psum | solution.py:208
  539.2 12.6 %copy-start.1 = (bf16[1,512,1024]{2,1,0:T(8,128)(2,1)S(1)}, bf16[1,512,1024]{2,1,0:T(8,128)(2,1)}, u32[]{:S(2)}) copy-start(bf16[1,512,1024]{2,1,0:T(8,128)(2,1)} %param.19) | copy-start | bytes 3145732
  539.2 12.6 %copy-start.11 = (bf16[512,3,2,1,512]{0,4,2,1,3:T(8,128)(2,1)S(1)}, bf16[512,3,2,1,512]{0,4,2,1,3:T(8,128)(2,1)}, u32[]{:S(2)}) copy-start(bf16[512,3,2,1,512]{0,4,2,1,3:T(8,128)(2,1)} %copy.89) | copy-start | bytes 9437188
  551.8 7.9 copy-start.22
  563.4 182.3 %copy-start.3 = (f32[512,1024]{1,0:T(8,128)S(1)}, f32[512,1024]{1,0:T(8,128)}, u32[]{:S(2)}) copy-start(f32[512,1024]{1,0:T(8,128)} %copy-done.2) | copy-start | bytes 6291460
  742.9 2.7 copy-start.7
  743.0 2.7 copy-start.9
  745.7 2.2 copy-start.23
Sparse Core Ops, SparseCore 0:
  10.4 64.7 all-gather.7
  77.3 40.1 all-gather.9
  119.6 72.9 all-gather.11
  194.7 72.9 all-gather.13
  309.1 70.6 reduce-scatter.9
  383.8 176.4 reduce-scatter.11
  564.4 176.4 reduce-scatter.13
  745.0 55.2 reduce-scatter.15
  804.3 134.0 reduce-scatter.7
  941.9 44.3 all-reduce.18
